TPU v7x, 256 devices: a whole 4x4x8 slice. The times are simulated.
256 devices in a mesh: frow: 8 (over z_lo, core), fcol: 32 (over x, z_hi, y).
Axes of the slice: x: 4, y: 4, z: 8 (z_hi: 2, z_lo: 4; z = z_hi * 4 + z_lo), core: 2. Of those that a mesh axis runs over, the one named last changes fastest.
Arguments:
- right_side: float32 [64, 1024, 256], P('frow', 'fcol'), may hold values from -6 to 6
- noise_weight: float32 [64, 1024, 256], P('frow', 'fcol'), may hold values from 3 to 4.5
- stencils: bfloat16 [9, 256, 256], replicated, may hold values from -1 to 1, as said below
- neighbours: int32 [64, 1024, 9], P('frow', 'fcol'), may hold values from -1 to 65535, as said below
Outputs:
- solution: float32 [64, 1024, 256], P('frow', 'fcol')
- coarse_residual: float32 [32, 512, 256], P('frow')
Inputs may be any that keep to these rules, and one draw needn't show every extreme that they name: `neighbours`: each entry is -1 (an empty slot) or the index r * 1024 + c of the tile at row r = own row + k // 3 - 1 and column c = own column + k % 3 - 1 for slot k; slot 4 always holds the tile itself; if tile t holds tile s in slot k, then s holds t in slot 8 - k. stencils[8 - k] is the transpose of stencils[k], and stencils[4] is symmetric.
All inputs are finite; a program needn't handle non-finite values.
Results may differ from a plain program's by a relative error of at most 0.0031.
Values may be sent and summed in bfloat16 or wider, within the bound.
A program may use at most 64 MiB of HBM per device.

v0:
```python
import jax
import jax.numpy as jnp
from jax import lax
from jax.sharding import PartitionSpec as P

DEG = 3


lower_edge = 1.5
upper_edge = 6.0


def with_halo(cells, sides, width):
    for axis, dim in sides:
        count = lax.axis_size(axis)
        ends = count - 1
        head = lax.slice_in_dim(cells, 0, width, axis=dim)
        tail = lax.slice_in_dim(cells, cells.shape[dim] - width, cells.shape[dim], axis=dim)
        cells = jnp.concatenate(
            [
                lax.ppermute(tail, axis, [(i, (i + 1) % count) for i in range(ends)]),
                cells,
                lax.ppermute(head, axis, [((i + 1) % count, i) for i in range(ends)]),
            ],
            axis=dim,
        )
    return cells


def restrict(paired_block):
    height, width, doubled = paired_block.shape
    pixels = doubled // 2
    summed = jnp.sum(paired_block.reshape(height // 2, 2, width, 2, pixels // 4, 4), axis=5)
    return jnp.transpose(summed, (0, 2, 1, 3, 4)).reshape(height // 2, width, pixels)


def smooth(right_side, operate):
    center = 0.5 * (upper_edge + lower_edge)
    half_width = 0.5 * (upper_edge - lower_edge)
    spread_ratio = center / half_width
    solution = jnp.zeros_like(right_side)
    residual = right_side
    for sweep_index in range(2):
        ratio_now = 1.0 / spread_ratio
        direction = residual / center
        for step_index in range(DEG):
            solution = solution + direction
            residual = residual - operate(direction)
            if step_index < DEG - 1:
                ratio_next = 1.0 / (2.0 * spread_ratio - ratio_now)
                direction = (
                    ratio_next * ratio_now * direction + 2.0 * ratio_next / half_width * residual
                )
                ratio_now = ratio_next
    return (solution, residual)


def body(right_side, noise_weight, stencils, neighbours):
    tile_rows, tile_cols, pixels = right_side.shape
    slots = stencils.shape[0]
    grid_cols = tile_cols * lax.axis_size("fcol")
    row_anchor = lax.axis_index("frow") * tile_rows
    col_anchor = lax.axis_index("fcol") * tile_cols
    padded_count = (tile_rows + 2) * (tile_cols + 2)
    local_row = neighbours // grid_cols - row_anchor + 1
    local_col = neighbours % grid_cols - col_anchor + 1
    targets = jnp.where(
        neighbours < 0, padded_count, local_row * (tile_cols + 2) + local_col
    ).reshape(-1)
    stencil_matrix = stencils.reshape(slots * pixels, pixels)

    def operate(direction):
        rounded = direction.astype(jnp.bfloat16)
        padded = with_halo(rounded, (("frow", 0), ("fcol", 1)), 1)
        flattened = jnp.concatenate(
            [padded.reshape(padded_count, pixels), jnp.zeros((1, pixels), jnp.bfloat16)], 0
        )
        picked = jnp.take(flattened, targets, axis=0).reshape(tile_rows * tile_cols, slots * pixels)
        coupled = jnp.dot(picked, stencil_matrix, preferred_element_type=jnp.float32)
        return noise_weight * direction + coupled.reshape(tile_rows, tile_cols, pixels)

    solution, residual = smooth(right_side, operate)
    paired = residual.reshape(tile_rows, tile_cols // 2, 2 * pixels)
    coarse_residual = lax.all_gather(restrict(paired), "fcol", axis=1, tiled=True)
    return (solution, coarse_residual)


def solution(mesh):
    placed = (P("frow", "fcol", None), P("frow", "fcol", None), P(), P("frow", "fcol", None))
    return jax.shard_map(
        body,
        mesh=mesh,
        in_specs=placed,
        out_specs=(P("frow", "fcol", None), P("frow", None, None)),
        check_vma=False,
    )
```

profile of v0, /device:TPU:1, one launch (start us, length us, event | category | flops | bytes accessed | tf_op | source)
XLA Modules:
  0.0 335.9 jit_solution(16433742648850729699)
XLA Ops:
  7.2 1.1 multiply_convert_fusion.1
  8.3 4.9 %collective-permute-start = (bf16[1,32,256]{2,1,0:T(8,128)(2,1)S(1)}, bf16[1,32,256]{2,1,0:T(8,128)(2,1)S(1)}, u32[]{:S(2)}, u32[]{:S(2)}) collective-permute-start(bf16[1,32,256]{2,1,0:T(8,128)(2,1)S(1)} %get-tuple-element.27), channel_id=1, source_target_pairs={{0,32},{32,64},{64,96},{96,128},{128,160},{160,192},{192,224},{1,3... | collective-permute-start | bytes 49160 | tf_op jit(solution)/shard_map/ppermute | solution.py:21
  13.2 1.9 collective-permute-start.1
  16.4 1.9 collective-permute-done.1
  18.3 3.2 collective-permute-start.2
  21.5 1.3 collective-permute-start.3
  22.8 3.1 collective-permute-done.3
  26.1 6.9 %gather_fusion = bf16[2304,256]{1,0:T(8,128)(2,1)S(1)} fusion(bf16[341,256]{1,0:T(8,128)(2,1)S(1)} %concatenate.56, s32[3072]{0:T(1024)S(1)} %pad_clamp_fusion), kind=kCustom, calls=%fused_computation.clone | custom fusion | bytes 2368512 | tf_op jit(solution)/shard_map/jit(_take)/gather | solution.py:78
  33.0 2.1 broadcast_select_fusion.5
  35.0 2.7 dot_general.30
  38.3 3.4 %collective-permute-start.4 = (bf16[1,32,256]{2,1,0:T(8,128)(2,1)S(1)}, bf16[1,32,256]{2,1,0:T(8,128)(2,1)S(1)}, u32[]{:S(2)}, u32[]{:S(2)}) collective-permute-start(bf16[1,32,256]{2,1,0:T(8,128)(2,1)S(1)} %get-tuple-element.25), channel_id=1, source_target_pairs={{0,32},{32,64},{64,96},{96,128},{128,160},{160,192},{192,224},{1,3... | collective-permute-start | bytes 49160 | tf_op jit(solution)/shard_map/ppermute | solution.py:21
  41.7 1.9 collective-permute-start.5
  43.6 3.1 collective-permute-done.5
  46.8 3.2 collective-permute-start.6
  50.0 1.3 collective-permute-start.7
  51.3 6.6 %collective-permute-done.7 = bf16[10,1,256]{2,1,0:T(2,128)(2,1)S(1)} collective-permute-done((bf16[10,1,256]{2,1,0:T(2,128)(2,1)S(1)}, bf16[10,1,256]{2,1,0:T(2,128)(2,1)S(1)}, u32[]{:S(2)}, u32[]{:S(2)}) %collective-permute-start.7) | collective-permute-done | bytes 5152 | tf_op jit(solution)/shard_map/ppermute | solution.py:23
  58.0 6.9 %gather_fusion.1 = bf16[2304,256]{1,0:T(8,128)(2,1)S(1)} fusion(bf16[341,256]{1,0:T(8,128)(2,1)S(1)} %concatenate.59, s32[3072]{0:T(1024)S(1)} %pad_clamp_fusion), kind=kCustom, calls=%fused_computation.1.clone | custom fusion | bytes 2368512 | tf_op jit(solution)/shard_map/jit(_take)/gather | solution.py:78
  64.9 2.1 broadcast_select_fusion.4
  67.0 2.7 dot_general.32
  69.6 1.2 fusion.6
  70.8 3.1 collective-permute-start.8
  73.9 1.9 collective-permute-start.9
  75.8 3.1 collective-permute-done.9
  79.0 9.7 %collective-permute-start.10 = (bf16[10,1,256]{2,1,0:T(2,128)(2,1)S(1)}, bf16[10,1,256]{2,1,0:T(2,128)(2,1)S(1)}, u32[]{:S(2)}, u32[]{:S(2)}) collective-permute-start(bf16[10,1,256]{2,1,0:T(2,128)(2,1)S(1)} %get-tuple-element.11), channel_id=1, source_target_pairs={{0,1},{1,2},{2,3},{3,4},{4,5},{5,6},{6,7},{7,8},{8,9},{9,10},{10,1... | collective-permute-start | bytes 15368 | tf_op jit(solution)/shard_map/ppermute | solution.py:21
  88.7 1.3 collective-permute-start.11
  90.0 3.4 %collective-permute-done.11 = bf16[10,1,256]{2,1,0:T(2,128)(2,1)S(1)} collective-permute-done((bf16[10,1,256]{2,1,0:T(2,128)(2,1)S(1)}, bf16[10,1,256]{2,1,0:T(2,128)(2,1)S(1)}, u32[]{:S(2)}, u32[]{:S(2)}) %collective-permute-start.11) | collective-permute-done | bytes 5152 | tf_op jit(solution)/shard_map/ppermute | solution.py:23
  93.5 7.5 %gather_fusion.2 = bf16[2304,256]{1,0:T(8,128)(2,1)} fusion(bf16[341,256]{1,0:T(8,128)(2,1)S(1)} %concatenate.62, s32[3072]{0:T(1024)S(1)} %pad_clamp_fusion), kind=kCustom, calls=%fused_computation.2.clone | custom fusion | bytes 2368512 | tf_op jit(solution)/shard_map/jit(_take)/gather | solution.py:78
  101.0 2.3 broadcast_select_fusion.3
  103.3 2.1 dot_general.34
  105.3 1.9 multiply_convert_fusion
  107.2 3.1 collective-permute-start.12
  110.3 1.9 collective-permute-start.13
  112.3 3.1 collective-permute-done.13
  115.4 7.7 %collective-permute-start.14 = (bf16[10,1,256]{2,1,0:T(2,128)(2,1)S(1)}, bf16[10,1,256]{2,1,0:T(2,128)(2,1)S(1)}, u32[]{:S(2)}, u32[]{:S(2)}) collective-permute-start(bf16[10,1,256]{2,1,0:T(2,128)(2,1)S(1)} %get-tuple-element.9), channel_id=1, source_target_pairs={{0,1},{1,2},{2,3},{3,4},{4,5},{5,6},{6,7},{7,8},{8,9},{9,10},{10,1... | collective-permute-start | bytes 15368 | tf_op jit(solution)/shard_map/ppermute | solution.py:21
  123.1 1.5 collective-permute-start.15
  124.6 3.2 collective-permute-done.15
  127.9 6.9 %gather_fusion.3 = bf16[2304,256]{1,0:T(8,128)(2,1)S(1)} fusion(bf16[341,256]{1,0:T(8,128)(2,1)S(1)} %concatenate.65, s32[3072]{0:T(1024)S(1)} %pad_clamp_fusion), kind=kCustom, calls=%fused_computation.3.clone | custom fusion | bytes 2368512 | tf_op jit(solution)/shard_map/jit(_take)/gather | solution.py:78
  134.8 2.1 broadcast_select_fusion.2
  136.9 2.7 dot_general.36
  139.5 1.2 fusion.20
  140.7 3.1 collective-permute-start.16
  143.8 1.9 collective-permute-start.17
  145.8 3.1 collective-permute-done.17
  148.9 7.7 %collective-permute-start.18 = (bf16[10,1,256]{2,1,0:T(2,128)(2,1)S(1)}, bf16[10,1,256]{2,1,0:T(2,128)(2,1)S(1)}, u32[]{:S(2)}, u32[]{:S(2)}) collective-permute-start(bf16[10,1,256]{2,1,0:T(2,128)(2,1)S(1)} %get-tuple-element.7), channel_id=1, source_target_pairs={{0,1},{1,2},{2,3},{3,4},{4,5},{5,6},{6,7},{7,8},{8,9},{9,10},{10,1... | collective-permute-start | bytes 15368 | tf_op jit(solution)/shard_map/ppermute | solution.py:21
  156.6 1.3 collective-permute-start.19
  157.9 3.4 %collective-permute-done.19 = bf16[10,1,256]{2,1,0:T(2,128)(2,1)S(1)} collective-permute-done((bf16[10,1,256]{2,1,0:T(2,128)(2,1)S(1)}, bf16[10,1,256]{2,1,0:T(2,128)(2,1)S(1)}, u32[]{:S(2)}, u32[]{:S(2)}) %collective-permute-start.19) | collective-permute-done | bytes 5152 | tf_op jit(solution)/shard_map/ppermute | solution.py:23
  161.4 6.9 %gather_fusion.4 = bf16[2304,256]{1,0:T(8,128)(2,1)S(1)} fusion(bf16[341,256]{1,0:T(8,128)(2,1)S(1)} %concatenate.68, s32[3072]{0:T(1024)S(1)} %pad_clamp_fusion), kind=kCustom, calls=%fused_computation.4.clone | custom fusion | bytes 2368512 | tf_op jit(solution)/shard_map/jit(_take)/gather | solution.py:78
  168.3 2.1 broadcast_select_fusion.1
  170.3 2.7 dot_general.38
  173.0 2.5 fusion.7
  175.5 3.1 collective-permute-start.20
  178.6 1.9 collective-permute-start.21
  180.5 3.1 collective-permute-done.21
  183.6 7.7 %collective-permute-start.22 = (bf16[10,1,256]{2,1,0:T(2,128)(2,1)S(1)}, bf16[10,1,256]{2,1,0:T(2,128)(2,1)S(1)}, u32[]{:S(2)}, u32[]{:S(2)}) collective-permute-start(bf16[10,1,256]{2,1,0:T(2,128)(2,1)S(1)} %get-tuple-element.5), channel_id=1, source_target_pairs={{0,1},{1,2},{2,3},{3,4},{4,5},{5,6},{6,7},{7,8},{8,9},{9,10},{10,1... | collective-permute-start | bytes 15368 | tf_op jit(solution)/shard_map/ppermute | solution.py:21
  191.3 1.5 collective-permute-start.23
  192.8 3.2 collective-permute-done.23
  196.2 6.9 %gather_fusion.5 = bf16[2304,256]{1,0:T(8,128)(2,1)S(1)} fusion(bf16[341,256]{1,0:T(8,128)(2,1)S(1)} %concatenate.71, s32[3072]{0:T(1024)S(1)} %pad_clamp_fusion), kind=kCustom, calls=%fused_computation.5.clone | custom fusion | bytes 2368512 | tf_op jit(solution)/shard_map/jit(_take)/gather | solution.py:78
  203.0 2.1 broadcast_select_fusion
  205.1 2.7 dot_general.40
  207.8 2.1 fusion
  210.0 10.9 %reshape_reshape.3 = f32[4,2,16,2,64,4]{5,4,3,2,1,0:T(8,128)} reshape(f32[8,32,256]{2,1,0:T(8,128)} %fusion) | data formatting | bytes 524288 | tf_op jit(solution)/shard_map/reshape;reshape | solution.py:33
  220.8 5.7 %reduce_sum.9 = f32[4,2,16,2,64]{4,3,2,1,0:T(2,128)S(1)} reduce(f32[4,2,16,2,64,4]{5,4,3,2,1,0:T(8,128)} %reshape_reshape.3, f32[]{:T(128)} %constant.74.clone.1), dimensions={5}, to_apply=%region_0.2 | reduce | flops 49152 | bytes 327684 | tf_op jit(solution)/shard_map/reduce_sum | solution.py:33
  227.4 98.6 %all-gather.2.cloned.1.call-done = f32[4,512,256]{2,1,0:T(8,128)} async-done(((f32[4,16,256]{2,1,0:T(8,128)}), f32[4,512,256]{2,1,0:T(8,128)}) %all-gather.2.cloned.1.call-update) | async-done | bytes 2097168 | tf_op jit(solution)/shard_map/all_gather | solution.py:84
  326.0 3.0 copy.11
  (63 shorter events, 3.6 us)
Async XLA Ops:
  7.2 30.6 %copy-start = (bf16[9,256,256]{2,1,0:T(8,128)(2,1)S(1)}, bf16[9,256,256]{2,1,0:T(8,128)(2,1)}, u32[]{:S(2)}) copy-start(bf16[9,256,256]{2,1,0:T(8,128)(2,1)} %param.8) | copy-start | bytes 3538948
  7.2 318.8 %all-gather.2.cloned.1.call-start = ((), (), s32[]{:S(2)}) async-start(), calls=%async_computation | async-start | bytes 2162688 | tf_op jit(solution)/shard_map/all_gather | solution.py:84
  8.3 8.0 %collective-permute-start = (bf16[1,32,256]{2,1,0:T(8,128)(2,1)S(1)}, bf16[1,32,256]{2,1,0:T(8,128)(2,1)S(1)}, u32[]{:S(2)}, u32[]{:S(2)}) collective-permute-start(bf16[1,32,256]{2,1,0:T(8,128)(2,1)S(1)} %get-tuple-element.27), channel_id=1, source_target_pairs={{0,32},{32,64},{64,96},{96,128},{128,160},{160,192},{192,224},{1,3... | collective-permute-start | bytes 49160 | tf_op jit(solution)/shard_map/ppermute | solution.py:21
  13.2 5.1 %collective-permute-start.1 = (bf16[1,32,256]{2,1,0:T(8,128)(2,1)S(1)}, bf16[1,32,256]{2,1,0:T(8,128)(2,1)S(1)}, u32[]{:S(2)}, u32[]{:S(2)}) collective-permute-start(bf16[1,32,256]{2,1,0:T(8,128)(2,1)S(1)} %get-tuple-element.28), channel_id=1, source_target_pairs={{32,0},{64,32},{96,64},{128,96},{160,128},{192,160},{224,192},{33,... | collective-permute-start | bytes 49160 | tf_op jit(solution)/shard_map/ppermute | solution.py:23
  18.3 4.5 %collective-permute-start.2 = (bf16[10,1,256]{2,1,0:T(2,128)(2,1)S(1)}, bf16[10,1,256]{2,1,0:T(2,128)(2,1)S(1)}, u32[]{:S(2)}, u32[]{:S(2)}) collective-permute-start(bf16[10,1,256]{2,1,0:T(2,128)(2,1)S(1)} %get-tuple-element.15), channel_id=1, source_target_pairs={{0,1},{1,2},{2,3},{3,4},{4,5},{5,6},{6,7},{7,8},{8,9},{9,10},{10,1... | collective-permute-start | bytes 15368 | tf_op jit(solution)/shard_map/ppermute | solution.py:21
  21.5 4.4 %collective-permute-start.3 = (bf16[10,1,256]{2,1,0:T(2,128)(2,1)S(1)}, bf16[10,1,256]{2,1,0:T(2,128)(2,1)S(1)}, u32[]{:S(2)}, u32[]{:S(2)}) collective-permute-start(bf16[10,1,256]{2,1,0:T(2,128)(2,1)S(1)} %get-tuple-element.16), channel_id=1, source_target_pairs={{1,0},{2,1},{3,2},{4,3},{5,4},{6,5},{7,6},{8,7},{9,8},{10,9},{11,1... | collective-permute-start | bytes 15368 | tf_op jit(solution)/shard_map/ppermute | solution.py:23
  35.0 2.7 copy-start.1
  35.0 2.7 copy-start.2
  38.3 31.3 %copy-start.3 = (f32[8,32,256]{2,1,0:T(8,128)}, f32[8,32,256]{2,1,0:T(8,128)S(1)}, u32[]{:S(2)}) copy-start(f32[8,32,256]{2,1,0:T(8,128)S(1)} %get-tuple-element.30) | copy-start | bytes 786436
  38.3 5.3 %collective-permute-start.4 = (bf16[1,32,256]{2,1,0:T(8,128)(2,1)S(1)}, bf16[1,32,256]{2,1,0:T(8,128)(2,1)S(1)}, u32[]{:S(2)}, u32[]{:S(2)}) collective-permute-start(bf16[1,32,256]{2,1,0:T(8,128)(2,1)S(1)} %get-tuple-element.25), channel_id=1, source_target_pairs={{0,32},{32,64},{64,96},{96,128},{128,160},{160,192},{192,224},{1,3... | collective-permute-start | bytes 49160 | tf_op jit(solution)/shard_map/ppermute | solution.py:21
  41.7 5.1 %collective-permute-start.5 = (bf16[1,32,256]{2,1,0:T(8,128)(2,1)S(1)}, bf16[1,32,256]{2,1,0:T(8,128)(2,1)S(1)}, u32[]{:S(2)}, u32[]{:S(2)}) collective-permute-start(bf16[1,32,256]{2,1,0:T(8,128)(2,1)S(1)} %get-tuple-element.26), channel_id=1, source_target_pairs={{32,0},{64,32},{96,64},{128,96},{160,128},{192,160},{224,192},{33,... | collective-permute-start | bytes 49160 | tf_op jit(solution)/shard_map/ppermute | solution.py:23
  46.8 4.5 %collective-permute-start.6 = (bf16[10,1,256]{2,1,0:T(2,128)(2,1)S(1)}, bf16[10,1,256]{2,1,0:T(2,128)(2,1)S(1)}, u32[]{:S(2)}, u32[]{:S(2)}) collective-permute-start(bf16[10,1,256]{2,1,0:T(2,128)(2,1)S(1)} %get-tuple-element.13), channel_id=1, source_target_pairs={{0,1},{1,2},{2,3},{3,4},{4,5},{5,6},{6,7},{7,8},{8,9},{9,10},{10,1... | collective-permute-start | bytes 15368 | tf_op jit(solution)/shard_map/ppermute | solution.py:21
  50.0 7.9 %collective-permute-start.7 = (bf16[10,1,256]{2,1,0:T(2,128)(2,1)S(1)}, bf16[10,1,256]{2,1,0:T(2,128)(2,1)S(1)}, u32[]{:S(2)}, u32[]{:S(2)}) collective-permute-start(bf16[10,1,256]{2,1,0:T(2,128)(2,1)S(1)} %get-tuple-element.14), channel_id=1, source_target_pairs={{1,0},{2,1},{3,2},{4,3},{5,4},{6,5},{7,6},{8,7},{9,8},{10,9},{11,1... | collective-permute-start | bytes 15368 | tf_op jit(solution)/shard_map/ppermute | solution.py:23
  70.8 5.0 %collective-permute-start.8 = (bf16[1,32,256]{2,1,0:T(8,128)(2,1)S(1)}, bf16[1,32,256]{2,1,0:T(8,128)(2,1)S(1)}, u32[]{:S(2)}, u32[]{:S(2)}) collective-permute-start(bf16[1,32,256]{2,1,0:T(8,128)(2,1)S(1)} %get-tuple-element.23), channel_id=1, source_target_pairs={{0,32},{32,64},{64,96},{96,128},{128,160},{160,192},{192,224},{1,3... | collective-permute-start | bytes 49160 | tf_op jit(solution)/shard_map/ppermute | solution.py:21
  73.9 5.1 %collective-permute-start.9 = (bf16[1,32,256]{2,1,0:T(8,128)(2,1)S(1)}, bf16[1,32,256]{2,1,0:T(8,128)(2,1)S(1)}, u32[]{:S(2)}, u32[]{:S(2)}) collective-permute-start(bf16[1,32,256]{2,1,0:T(8,128)(2,1)S(1)} %get-tuple-element.24), channel_id=1, source_target_pairs={{32,0},{64,32},{96,64},{128,96},{160,128},{192,160},{224,192},{33,... | collective-permute-start | bytes 49160 | tf_op jit(solution)/shard_map/ppermute | solution.py:23
  79.0 11.0 %collective-permute-start.10 = (bf16[10,1,256]{2,1,0:T(2,128)(2,1)S(1)}, bf16[10,1,256]{2,1,0:T(2,128)(2,1)S(1)}, u32[]{:S(2)}, u32[]{:S(2)}) collective-permute-start(bf16[10,1,256]{2,1,0:T(2,128)(2,1)S(1)} %get-tuple-element.11), channel_id=1, source_target_pairs={{0,1},{1,2},{2,3},{3,4},{4,5},{5,6},{6,7},{7,8},{8,9},{9,10},{10,1... | collective-permute-start | bytes 15368 | tf_op jit(solution)/shard_map/ppermute | solution.py:21
  88.7 4.7 %collective-permute-start.11 = (bf16[10,1,256]{2,1,0:T(2,128)(2,1)S(1)}, bf16[10,1,256]{2,1,0:T(2,128)(2,1)S(1)}, u32[]{:S(2)}, u32[]{:S(2)}) collective-permute-start(bf16[10,1,256]{2,1,0:T(2,128)(2,1)S(1)} %get-tuple-element.12), channel_id=1, source_target_pairs={{1,0},{2,1},{3,2},{4,3},{5,4},{6,5},{7,6},{8,7},{9,8},{10,9},{11,1... | collective-permute-start | bytes 15368 | tf_op jit(solution)/shard_map/ppermute | solution.py:23
  107.2 5.0 %collective-permute-start.12 = (bf16[1,32,256]{2,1,0:T(8,128)(2,1)S(1)}, bf16[1,32,256]{2,1,0:T(8,128)(2,1)S(1)}, u32[]{:S(2)}, u32[]{:S(2)}) collective-permute-start(bf16[1,32,256]{2,1,0:T(8,128)(2,1)S(1)} %get-tuple-element.21), channel_id=1, source_target_pairs={{0,32},{32,64},{64,96},{96,128},{128,160},{160,192},{192,224},{1,3... | collective-permute-start | bytes 49160 | tf_op jit(solution)/shard_map/ppermute | solution.py:21
  110.3 5.1 %collective-permute-start.13 = (bf16[1,32,256]{2,1,0:T(8,128)(2,1)S(1)}, bf16[1,32,256]{2,1,0:T(8,128)(2,1)S(1)}, u32[]{:S(2)}, u32[]{:S(2)}) collective-permute-start(bf16[1,32,256]{2,1,0:T(8,128)(2,1)S(1)} %get-tuple-element.22), channel_id=1, source_target_pairs={{32,0},{64,32},{96,64},{128,96},{160,128},{192,160},{224,192},{33,... | collective-permute-start | bytes 49160 | tf_op jit(solution)/shard_map/ppermute | solution.py:23
  115.4 9.1 %collective-permute-start.14 = (bf16[10,1,256]{2,1,0:T(2,128)(2,1)S(1)}, bf16[10,1,256]{2,1,0:T(2,128)(2,1)S(1)}, u32[]{:S(2)}, u32[]{:S(2)}) collective-permute-start(bf16[10,1,256]{2,1,0:T(2,128)(2,1)S(1)} %get-tuple-element.9), channel_id=1, source_target_pairs={{0,1},{1,2},{2,3},{3,4},{4,5},{5,6},{6,7},{7,8},{8,9},{9,10},{10,1... | collective-permute-start | bytes 15368 | tf_op jit(solution)/shard_map/ppermute | solution.py:21
  123.1 4.7 %collective-permute-start.15 = (bf16[10,1,256]{2,1,0:T(2,128)(2,1)S(1)}, bf16[10,1,256]{2,1,0:T(2,128)(2,1)S(1)}, u32[]{:S(2)}, u32[]{:S(2)}) collective-permute-start(bf16[10,1,256]{2,1,0:T(2,128)(2,1)S(1)} %get-tuple-element.10), channel_id=1, source_target_pairs={{1,0},{2,1},{3,2},{4,3},{5,4},{6,5},{7,6},{8,7},{9,8},{10,9},{11,1... | collective-permute-start | bytes 15368 | tf_op jit(solution)/shard_map/ppermute | solution.py:23
  140.7 5.0 %collective-permute-start.16 = (bf16[1,32,256]{2,1,0:T(8,128)(2,1)S(1)}, bf16[1,32,256]{2,1,0:T(8,128)(2,1)S(1)}, u32[]{:S(2)}, u32[]{:S(2)}) collective-permute-start(bf16[1,32,256]{2,1,0:T(8,128)(2,1)S(1)} %get-tuple-element.19), channel_id=1, source_target_pairs={{0,32},{32,64},{64,96},{96,128},{128,160},{160,192},{192,224},{1,3... | collective-permute-start | bytes 49160 | tf_op jit(solution)/shard_map/ppermute | solution.py:21
  143.8 5.1 %collective-permute-start.17 = (bf16[1,32,256]{2,1,0:T(8,128)(2,1)S(1)}, bf16[1,32,256]{2,1,0:T(8,128)(2,1)S(1)}, u32[]{:S(2)}, u32[]{:S(2)}) collective-permute-start(bf16[1,32,256]{2,1,0:T(8,128)(2,1)S(1)} %get-tuple-element.20), channel_id=1, source_target_pairs={{32,0},{64,32},{96,64},{128,96},{160,128},{192,160},{224,192},{33,... | collective-permute-start | bytes 49160 | tf_op jit(solution)/shard_map/ppermute | solution.py:23
  148.9 9.0 %collective-permute-start.18 = (bf16[10,1,256]{2,1,0:T(2,128)(2,1)S(1)}, bf16[10,1,256]{2,1,0:T(2,128)(2,1)S(1)}, u32[]{:S(2)}, u32[]{:S(2)}) collective-permute-start(bf16[10,1,256]{2,1,0:T(2,128)(2,1)S(1)} %get-tuple-element.7), channel_id=1, source_target_pairs={{0,1},{1,2},{2,3},{3,4},{4,5},{5,6},{6,7},{7,8},{8,9},{9,10},{10,1... | collective-permute-start | bytes 15368 | tf_op jit(solution)/shard_map/ppermute | solution.py:21
  156.6 4.7 %collective-permute-start.19 = (bf16[10,1,256]{2,1,0:T(2,128)(2,1)S(1)}, bf16[10,1,256]{2,1,0:T(2,128)(2,1)S(1)}, u32[]{:S(2)}, u32[]{:S(2)}) collective-permute-start(bf16[10,1,256]{2,1,0:T(2,128)(2,1)S(1)} %get-tuple-element.8), channel_id=1, source_target_pairs={{1,0},{2,1},{3,2},{4,3},{5,4},{6,5},{7,6},{8,7},{9,8},{10,9},{11,1... | collective-permute-start | bytes 15368 | tf_op jit(solution)/shard_map/ppermute | solution.py:23
  175.5 5.0 %collective-permute-start.20 = (bf16[1,32,256]{2,1,0:T(8,128)(2,1)S(1)}, bf16[1,32,256]{2,1,0:T(8,128)(2,1)S(1)}, u32[]{:S(2)}, u32[]{:S(2)}) collective-permute-start(bf16[1,32,256]{2,1,0:T(8,128)(2,1)S(1)} %get-tuple-element.17), channel_id=1, source_target_pairs={{0,32},{32,64},{64,96},{96,128},{128,160},{160,192},{192,224},{1,3... | collective-permute-start | bytes 49160 | tf_op jit(solution)/shard_map/ppermute | solution.py:21
  178.6 5.1 %collective-permute-start.21 = (bf16[1,32,256]{2,1,0:T(8,128)(2,1)S(1)}, bf16[1,32,256]{2,1,0:T(8,128)(2,1)S(1)}, u32[]{:S(2)}, u32[]{:S(2)}) collective-permute-start(bf16[1,32,256]{2,1,0:T(8,128)(2,1)S(1)} %get-tuple-element.18), channel_id=1, source_target_pairs={{32,0},{64,32},{96,64},{128,96},{160,128},{192,160},{224,192},{33,... | collective-permute-start | bytes 49160 | tf_op jit(solution)/shard_map/ppermute | solution.py:23
  183.6 9.2 %collective-permute-start.22 = (bf16[10,1,256]{2,1,0:T(2,128)(2,1)S(1)}, bf16[10,1,256]{2,1,0:T(2,128)(2,1)S(1)}, u32[]{:S(2)}, u32[]{:S(2)}) collective-permute-start(bf16[10,1,256]{2,1,0:T(2,128)(2,1)S(1)} %get-tuple-element.5), channel_id=1, source_target_pairs={{0,1},{1,2},{2,3},{3,4},{4,5},{5,6},{6,7},{7,8},{8,9},{9,10},{10,1... | collective-permute-start | bytes 15368 | tf_op jit(solution)/shard_map/ppermute | solution.py:21
  191.3 4.7 %collective-permute-start.23 = (bf16[10,1,256]{2,1,0:T(2,128)(2,1)S(1)}, bf16[10,1,256]{2,1,0:T(2,128)(2,1)S(1)}, u32[]{:S(2)}, u32[]{:S(2)}) collective-permute-start(bf16[10,1,256]{2,1,0:T(2,128)(2,1)S(1)} %get-tuple-element.6), channel_id=1, source_target_pairs={{1,0},{2,1},{3,2},{4,3},{5,4},{6,5},{7,6},{8,7},{9,8},{10,9},{11,1... | collective-permute-start | bytes 15368 | tf_op jit(solution)/shard_map/ppermute | solution.py:23
  205.1 2.7 copy-start.4
Sparse Core Ops, SparseCore 0:
  227.5 98.4 all-gather.1
where the time goes:
time: 341 us; the launch traced here: 336 us
  waiting for transfers between devices  139 us (41%)
  starting transfers between devices  79.3 us (23%)
  local copies, waits for them, and re-layouts  72.8 us (21%)
  other arithmetic  20.7 us (6%)
  between operations  14.7 us (4%)
  matrix products  9.38 us (3%)
    all_gather x1, waiting for transfers between devices, body(): lax.all_gather(restrict(paired), 'fcol', axis=1, tiled=True)  98.6 us
    ppermute x12, starting transfers between devices, with_halo(): lax.ppermute(tail, axis, [(i, (i + 1) % count) for i in range(ends)])  59.6 us
    gather x6, local copies, waits for them, and re-layouts, operate(): jnp.take(flattened, targets, axis=0)  41.8 us
    ppermute x12, waiting for transfers between devices, with_halo(): lax.ppermute(head, axis, [((i + 1) % count, i) for i in range(ends)])  40.4 us
    ppermute x12, starting transfers between devices, with_halo(): lax.ppermute(head, axis, [((i + 1) % count, i) for i in range(ends)])  19.7 us
    dot_general x6, local copies, waits for them, and re-layouts, operate(): jnp.dot(picked, stencil_matrix, preferred_element_type=jnp.float32)  15.5 us
    select_n x7, other arithmetic, operate(): jnp.take(flattened, targets, axis=0)  12.6 us
    another operation x1, local copies, waits for them, and re-layouts, restrict(): paired_block.reshape(height // 2, 2, width, 2, pixels // 4, 4)  10.9 us
  transfers between devices with their start and end apart: 25, of which 13 were waited for; matrix products, arithmetic and copies ran while one was open for 0% of the time, Pallas kernels for 0%

commit v1 on v0

v1 whole, which is shorter than its diff:
```python
import functools

import jax
import jax.numpy as jnp
from jax import lax
from jax.experimental import pallas as pl
from jax.experimental.pallas import tpu as pltpu
from jax.sharding import PartitionSpec as P

MESH = pl.DeviceIdType.MESH
LOWER, UPPER, DEG, SWEEPS = 1.5, 6.0, 3, 2
HALO = DEG * SWEEPS
SIDE = 8


def coefficients():
    center = 0.5 * (UPPER + LOWER)
    half_width = 0.5 * (UPPER - LOWER)
    spread = center / half_width
    steps = []
    for _ in range(SWEEPS):
        ratio = 1.0 / spread
        for step in range(DEG):
            if step < DEG - 1:
                after = 1.0 / (2.0 * spread - ratio)
                steps.append((after * ratio, 2.0 * after / half_width))
                ratio = after
            else:
                steps.append((0.0, 1.0 / center))
    return center, steps


def kernel(
    sizes, rs, nw, st, nb, sol_ref, out_ref, res, wgt, drc, dir_bf, msk, nbx, stv, fin, halo_send, halo_recv, loc_sem, g_send, g_recv
):
    n_row, n_col, rows, cols, pix, slots = sizes
    ext_rows, ext_cols = rows + 2 * HALO, cols + 2 * SIDE
    frow, fcol = lax.axis_index("frow"), lax.axis_index("fcol")

    def at(dr, dc):
        return (lax.rem(frow + (dr + n_row), n_row), lax.rem(fcol + (dc + n_col), n_col))

    local = [
        pltpu.make_async_copy(nb, nbx.at[4], loc_sem.at[0]),
        pltpu.make_async_copy(rs, res.at[pl.ds(HALO, rows), pl.ds(SIDE, cols)], loc_sem.at[1]),
        pltpu.make_async_copy(nw, wgt.at[pl.ds(HALO, rows), pl.ds(SIDE, cols)], loc_sem.at[2]),
        pltpu.make_async_copy(st, stv, loc_sem.at[3]),
    ]
    for copy in local:
        copy.start()

    barrier = pltpu.get_barrier_semaphore()
    for dr in (-1, 1):
        for dc in (-1, 0, 1):
            pl.semaphore_signal(barrier, inc=1, device_id=at(dr, dc), device_id_type=MESH)

    def hail(i, c):
        pl.semaphore_signal(barrier, inc=1, device_id=(frow, lax.rem(fcol + i, n_col)), device_id_type=MESH)
        return c

    lax.fori_loop(1, n_col, hail, 0)
    pl.semaphore_wait(barrier, 6 + n_col - 1)

    halo = {}
    for dr in (-1, 0, 1):
        for dc in (-1, 0, 1):
            if dr == 0 and dc == 0:
                continue
            src_r = {-1: pl.ds(0, HALO), 0: pl.ds(0, rows), 1: pl.ds(rows - HALO, HALO)}[dr]
            dst_r = {-1: pl.ds(HALO + rows, HALO), 0: pl.ds(HALO, rows), 1: pl.ds(0, HALO)}[dr]
            src_c = {-1: pl.ds(0, SIDE), 0: pl.ds(0, cols), 1: pl.ds(cols - SIDE, SIDE)}[dc]
            dst_c = {-1: pl.ds(SIDE + cols, SIDE), 0: pl.ds(SIDE, cols), 1: pl.ds(0, SIDE)}[dc]
            slot = (1 - dr) * 3 + (1 - dc)
            index = slot if slot < 4 else slot - 1
            trio = []
            for j, (src, dst) in enumerate(
                (
                    (nb, nbx.at[slot]),
                    (rs.at[src_r, src_c], res.at[dst_r, dst_c]),
                    (nw.at[src_r, src_c], wgt.at[dst_r, dst_c]),
                )
            ):
                copy = pltpu.make_async_remote_copy(
                    src_ref=src,
                    dst_ref=dst,
                    send_sem=halo_send.at[index * 3 + j],
                    recv_sem=halo_recv.at[index * 3 + j],
                    device_id=at(dr, dc),
                    device_id_type=MESH,
                )
                trio.append(copy)
            halo[dr, dc] = trio
    for key in ((0, 1), (0, -1), (1, 1), (1, -1), (-1, 1), (-1, -1), (1, 0), (-1, 0)):
        for copy in halo[key]:
            copy.start()
    for copy in local:
        copy.wait()
    for key in halo:
        for copy in halo[key]:
            copy.wait()

    for block, first, last, base in ((0, rows - HALO, rows, 0), (1, 0, rows, HALO), (2, 0, HALO, HALO + rows)):
        def turned(slot):
            flat = jnp.where(nbx[slot] >= 0, 1.0, 0.0).astype(jnp.float32).reshape(slots * rows, cols)
            return jnp.transpose(flat)

        whole = jnp.concatenate(
            [turned(3 * block)[cols - SIDE :], turned(3 * block + 1), turned(3 * block + 2)[:SIDE]], axis=0
        )
        for k in range(slots):
            for row in range(first, last):
                m = k * rows + row
                wide = jnp.broadcast_to(whole[:, m : m + 1], (ext_cols, 128)).astype(jnp.bfloat16)
                msk[k, pl.ds((base + row - first) * ext_cols, ext_cols), :] = wide

    center, steps = coefficients()

    def put(buf, t0, count, value):
        for j, shift in enumerate((1, 0, count - 1)):
            moved = value if shift == 0 else pltpu.roll(value, shift, axis=0)
            dir_bf[buf, j, pl.ds(t0, count), :] = moved.astype(jnp.bfloat16)

    res_flat = res.reshape(ext_rows * ext_cols, pix)
    wgt_flat = wgt.reshape(ext_rows * ext_cols, pix)

    def begin(i, c):
        t0 = pl.multiple_of(i * (2 * ext_cols), 2 * ext_cols)
        d = res_flat[pl.ds(t0, 2 * ext_cols), :] * (1.0 / center)
        drc[pl.ds(t0, 2 * ext_cols), :] = d
        put(0, t0, 2 * ext_cols, d)
        return c

    lax.fori_loop(0, ext_rows // 2, begin, 0)

    drc_cube = drc.reshape(ext_rows, ext_cols, pix)

    for op in range(HALO):
        now, later = op % 2, (op + 1) % 2
        low = op + 1
        count = ext_rows - 2 * low
        chunk = CHUNK[op]
        size = chunk * ext_cols
        own = drc_cube[pl.ds(HALO, rows), pl.ds(SIDE, cols), :]
        sol_ref[...] = own if op == 0 else sol_ref[...] + own

        def apply(i, c, now=now, later=later, low=low, size=size, op=op):
            t0 = pl.multiple_of(low * ext_cols + i * size, ext_cols)
            parts = []
            for k in range(slots):
                src = t0 + (k // 3 - 1) * ext_cols
                part = dir_bf[now, k % 3, pl.ds(pl.multiple_of(src, ext_cols), size), :]
                keep = msk[k, pl.ds(t0, size), :]
                parts.append(part * jnp.concatenate([keep, keep], axis=1))
            coupled = jnp.dot(
                jnp.concatenate(parts, axis=1), stv[...].reshape(slots * pix, pix), preferred_element_type=jnp.float32
            )
            d = drc[pl.ds(t0, size), :]
            r = res_flat[pl.ds(t0, size), :] - (wgt_flat[pl.ds(t0, size), :] * d + coupled)
            if op == HALO - 1:
                for h in range(pix // 128):
                    fin[h] = r[:, h * 128 : (h + 1) * 128]
            else:
                res_flat[pl.ds(t0, size), :] = r
                old, new = steps[op]
                d = new * r if old == 0.0 else old * d + new * r
                drc[pl.ds(t0, size), :] = d
                put(later, t0, size, d)
            return c

        trips = count // chunk
        if trips == 1:
            apply(0, 0)
        else:
            lax.fori_loop(0, trips, apply, 0)

    pixel = lax.broadcasted_iota(jnp.int32, (pix, 128), 0)
    lane = lax.broadcasted_iota(jnp.int32, (pix, 128), 1)
    fold = jnp.where(pixel // 4 == lane % 64, 1.0, 0.0).astype(jnp.bfloat16)
    pieces = []
    for a in range(2):
        for b in range(2):
            for R in range(rows // 2):
                begin_at = (2 * R + a) * ext_cols + SIDE + b
                pieces.append(
                    jnp.concatenate(
                        [fin[h, pl.ds(begin_at, cols // 2, stride=2), :] for h in range(pix // 128)], axis=1
                    )
                )
    stack = jnp.concatenate(pieces, axis=0)
    high = stack.astype(jnp.bfloat16)
    low_part = (stack - high.astype(jnp.float32)).astype(jnp.bfloat16)
    summed = jnp.dot(high, fold, preferred_element_type=jnp.float32) + jnp.dot(
        low_part, fold, preferred_element_type=jnp.float32
    )
    quarter = (rows // 2) * (cols // 2)
    y = [summed[q * quarter : (q + 1) * quarter] for q in range(4)]
    left = lax.broadcasted_iota(jnp.int32, (quarter, 128), 1) < 64
    coarse = jnp.concatenate([jnp.where(left, y[0], y[1]), jnp.where(left, y[2], y[3])], axis=1).astype(jnp.bfloat16)
    mine = pl.ds(pl.multiple_of(fcol * (cols // 2), cols // 2), cols // 2)
    out_ref[:, mine, :] = coarse.reshape(rows // 2, cols // 2, pix)

    def given(i):
        return pltpu.make_async_remote_copy(
            src_ref=out_ref.at[:, mine, :],
            dst_ref=out_ref.at[:, mine, :],
            send_sem=g_send.at[i],
            recv_sem=g_recv.at[i],
            device_id=(frow, lax.rem(fcol + i, n_col)),
            device_id_type=MESH,
        )

    def start(i, c):
        given(i).start()
        return c

    def finish(i, c):
        other = lax.rem(fcol - i + n_col, n_col)
        theirs = pl.ds(pl.multiple_of(other * (cols // 2), cols // 2), cols // 2)
        pltpu.make_async_remote_copy(
            src_ref=out_ref.at[:, theirs, :],
            dst_ref=out_ref.at[:, theirs, :],
            send_sem=g_send.at[i],
            recv_sem=g_recv.at[i],
            device_id=(frow, lax.rem(fcol + i, n_col)),
            device_id_type=MESH,
        ).wait_recv()
        given(i).wait_send()
        return c

    lax.fori_loop(1, n_col, start, 0)
    lax.fori_loop(1, n_col, finish, 0)


CHUNK = (9, 8, 7, 6, 5, 8)


def solution(mesh):
    n_row, n_col = mesh.shape["frow"], mesh.shape["fcol"]

    def body(right_side, noise_weight, stencils, neighbours):
        rows, cols, pix = right_side.shape
        slots = stencils.shape[0]
        ext = (rows + 2 * HALO, cols + 2 * SIDE)
        tiles = ext[0] * ext[1]
        listed = jnp.transpose(neighbours, (2, 0, 1))
        smooth, coarse = pl.pallas_call(
            functools.partial(kernel, (n_row, n_col, rows, cols, pix, slots)),
            out_shape=(
                jax.ShapeDtypeStruct((rows, cols, pix), jnp.float32),
                jax.ShapeDtypeStruct((rows // 2, cols // 2 * n_col, pix), jnp.bfloat16),
            ),
            in_specs=[pl.BlockSpec(memory_space=pl.ANY)] * 4,
            out_specs=(pl.BlockSpec(memory_space=pltpu.VMEM), pl.BlockSpec(memory_space=pltpu.VMEM)),
            scratch_shapes=[
                pltpu.VMEM(ext + (pix,), jnp.float32),
                pltpu.VMEM(ext + (pix,), jnp.float32),
                pltpu.VMEM((tiles, pix), jnp.float32),
                pltpu.VMEM((2, 3, tiles, pix), jnp.bfloat16),
                pltpu.VMEM((slots, tiles, 128), jnp.bfloat16),
                pltpu.VMEM((9, slots, rows, cols), jnp.int32),
                pltpu.VMEM((slots, pix, pix), jnp.bfloat16),
                pltpu.VMEM((pix // 128, rows * ext[1], 128), jnp.float32),
                pltpu.SemaphoreType.DMA((24,)),
                pltpu.SemaphoreType.DMA((24,)),
                pltpu.SemaphoreType.DMA((4,)),
                pltpu.SemaphoreType.DMA((n_col,)),
                pltpu.SemaphoreType.DMA((n_col,)),
            ],
            compiler_params=pltpu.CompilerParams(
                collective_id=0, has_side_effects=True, vmem_limit_bytes=48 << 20
            ),
        )(right_side, noise_weight, stencils, listed)
        return smooth, coarse.astype(jnp.float32)

    placed = (P("frow", "fcol", None), P("frow", "fcol", None), P(), P("frow", "fcol", None))
    return jax.shard_map(
        body,
        mesh=mesh,
        in_specs=placed,
        out_specs=(P("frow", "fcol", None), P("frow", None, None)),
        check_vma=False,
    )
```

time: 341 us -> 82.6 us (0.24)
  the two profiles are of different devices: /device:TPU:1 before, /device:TPU:121 now
where the time goes in v1:
time: 82.6 us; the launch traced here: 82.3 us
  Pallas kernels  75.5 us (91%)
  local copies, waits for them, and re-layouts  4.63 us (6%)
  other arithmetic  1.5 us (2%)
    pallas_call x1, Pallas kernels, body(): pl.pallas_call(functools.partial(kernel, (n_row, n_col, rows, cols, pix,...  75.5 us
    unnamed x9, local copies, waits for them, and re-layouts  4.63 us

profile of v1, /device:TPU:121, one launch (start us, length us, event | category | flops | bytes accessed | tf_op | source)
XLA Modules:
  0.0 82.3 jit_solution(12448443937943069381)
XLA Ops:
  0.6 0.0 copy-start
  0.6 1.3 %copy-done = bf16[9,256,256]{2,1,0:T(8,128)(2,1)S(1)} copy-done((bf16[9,256,256]{2,1,0:T(8,128)(2,1)S(1)}, bf16[9,256,256]{2,1,0:T(8,128)(2,1)}, u32[]{:S(2)}) %copy-start) | copy-done | bytes 1179672
  1.9 0.0 copy-start.1
  1.9 0.9 %copy-done.1 = f32[8,32,256]{2,1,0:T(8,128)S(1)} copy-done((f32[8,32,256]{2,1,0:T(8,128)S(1)}, f32[8,32,256]{2,1,0:T(8,128)}, u32[]{:S(2)}) %copy-start.1) | copy-done | bytes 262168
  2.9 0.0 copy-start.2
  2.9 0.9 %copy-done.2 = f32[8,32,256]{2,1,0:T(8,128)S(1)} copy-done((f32[8,32,256]{2,1,0:T(8,128)S(1)}, f32[8,32,256]{2,1,0:T(8,128)}, u32[]{:S(2)}) %copy-start.2) | copy-done | bytes 262168
  3.8 0.0 copy-start.3
  3.8 0.8 copy-done.3
  4.6 75.5 %shard_map.59 = (f32[8,32,256]{2,1,0:T(8,128)S(1)}, bf16[4,512,256]{2,1,0:T(8,128)(2,1)S(1)}) custom-call(f32[8,32,256]{2,1,0:T(8,128)S(1)} %copy-done.1, f32[8,32,256]{2,1,0:T(8,128)S(1)} %copy-done.2, bf16[9,256,256]{2,1,0:T(8,128)(2,1)S(1)} %copy-done, s32[9,8,32]{2,1,0:T(8,128)S(1)} %bitcast.1), custom_call_target="tpu_custom_call" | custom-call | tf_op jit(solution)/shard_map/pallas_call | solution.py:246
  80.1 1.5 %convert_element_type.3 = f32[4,512,256]{2,1,0:T(8,128)} convert(bf16[4,512,256]{2,1,0:T(8,128)(2,1)S(1)} %get-tuple-element.5) | non-fusion elementwise | flops 524288 | bytes 3145728 | tf_op jit(solution)/shard_map/convert_element_type | solution.py:273
  81.6 0.7 copy.7
Async XLA Ops:
  0.6 1.3 %copy-start = (bf16[9,256,256]{2,1,0:T(8,128)(2,1)S(1)}, bf16[9,256,256]{2,1,0:T(8,128)(2,1)}, u32[]{:S(2)}) copy-start(bf16[9,256,256]{2,1,0:T(8,128)(2,1)} %st.1) | copy-start | bytes 3538948
  1.9 0.9 %copy-start.1 = (f32[8,32,256]{2,1,0:T(8,128)S(1)}, f32[8,32,256]{2,1,0:T(8,128)}, u32[]{:S(2)}) copy-start(f32[8,32,256]{2,1,0:T(8,128)} %rs.1) | copy-start | bytes 786436
  2.9 0.9 %copy-start.2 = (f32[8,32,256]{2,1,0:T(8,128)S(1)}, f32[8,32,256]{2,1,0:T(8,128)}, u32[]{:S(2)}) copy-start(f32[8,32,256]{2,1,0:T(8,128)} %nw.1) | copy-start | bytes 786436
  3.8 0.8 copy-start.3

commit v2 on v1

--- a/solution.py
+++ b/solution.py
@@ -11,6 +11,7 @@
 LOWER, UPPER, DEG, SWEEPS = 1.5, 6.0, 3, 2
 HALO = DEG * SWEEPS
 SIDE = 8
+MIDDLE = 3.75
 
 
 def coefficients():
@@ -31,17 +32,38 @@
 
 
 def kernel(
-    sizes, rs, nw, st, nb, sol_ref, out_ref, res, wgt, drc, dir_bf, msk, nbx, stv, fin, halo_send, halo_recv, loc_sem, g_send, g_recv
+    sizes, rs, nw, st, nb, sol_ref, out_ref, res, wgt, drc, dir_bf, msk, fin, own_nb, stv,
+    band_out, band_in, strip_out, strip_in, corner_in, loc_sem, h_send, h_recv, g_send, g_recv
 ):
     n_row, n_col, rows, cols, pix, slots = sizes
     ext_rows, ext_cols = rows + 2 * HALO, cols + 2 * SIDE
     frow, fcol = lax.axis_index("frow"), lax.axis_index("fcol")
-
-    def at(dr, dc):
-        return (lax.rem(frow + (dr + n_row), n_row), lax.rem(fcol + (dc + n_col), n_col))
+    f32, bf16 = jnp.float32, jnp.bfloat16
+    has = {"up": frow > 0, "down": frow < n_row - 1, "left": fcol > 0, "right": fcol < n_col - 1}
+    beside = {"up": (frow - 1, fcol), "down": (frow + 1, fcol), "left": (frow, fcol - 1), "right": (frow, fcol + 1)}
+    sides = ("up", "down", "left", "right")
+    y, zh = lax.rem(fcol, 4), lax.rem(fcol // 4, 2)
+
+    def along_x(d):
+        return lax.rem(fcol + 8 * d, n_col)
+
+    def along_y(d):
+        return fcol - y + lax.rem(y + d, 4)
+
+    partner = fcol + 4 - 8 * zh
+
+    barrier = pltpu.get_barrier_semaphore()
+    for side in sides:
+
+        @pl.when(has[side])
+        def _(side=side):
+            pl.semaphore_signal(barrier, inc=1, device_id=beside[side], device_id_type=MESH)
+
+    for peer in [along_x(d) for d in (1, 2, 3)] + [along_y(d) for d in (1, 2, 3)] + [partner]:
+        pl.semaphore_signal(barrier, inc=1, device_id=(frow, peer), device_id_type=MESH)
 
     local = [
-        pltpu.make_async_copy(nb, nbx.at[4], loc_sem.at[0]),
+        pltpu.make_async_copy(nb, own_nb, loc_sem.at[0]),
         pltpu.make_async_copy(rs, res.at[pl.ds(HALO, rows), pl.ds(SIDE, cols)], loc_sem.at[1]),
         pltpu.make_async_copy(nw, wgt.at[pl.ds(HALO, rows), pl.ds(SIDE, cols)], loc_sem.at[2]),
         pltpu.make_async_copy(st, stv, loc_sem.at[3]),
@@ -49,69 +71,137 @@
     for copy in local:
         copy.start()
 
-    barrier = pltpu.get_barrier_semaphore()
-    for dr in (-1, 1):
-        for dc in (-1, 0, 1):
-            pl.semaphore_signal(barrier, inc=1, device_id=at(dr, dc), device_id_type=MESH)
-
-    def hail(i, c):
-        pl.semaphore_signal(barrier, inc=1, device_id=(frow, lax.rem(fcol + i, n_col)), device_id_type=MESH)
-        return c
-
-    lax.fori_loop(1, n_col, hail, 0)
-    pl.semaphore_wait(barrier, 6 + n_col - 1)
-
-    halo = {}
-    for dr in (-1, 0, 1):
-        for dc in (-1, 0, 1):
-            if dr == 0 and dc == 0:
-                continue
-            src_r = {-1: pl.ds(0, HALO), 0: pl.ds(0, rows), 1: pl.ds(rows - HALO, HALO)}[dr]
-            dst_r = {-1: pl.ds(HALO + rows, HALO), 0: pl.ds(HALO, rows), 1: pl.ds(0, HALO)}[dr]
-            src_c = {-1: pl.ds(0, SIDE), 0: pl.ds(0, cols), 1: pl.ds(cols - SIDE, SIDE)}[dc]
-            dst_c = {-1: pl.ds(SIDE + cols, SIDE), 0: pl.ds(SIDE, cols), 1: pl.ds(0, SIDE)}[dc]
-            slot = (1 - dr) * 3 + (1 - dc)
-            index = slot if slot < 4 else slot - 1
-            trio = []
-            for j, (src, dst) in enumerate(
-                (
-                    (nb, nbx.at[slot]),
-                    (rs.at[src_r, src_c], res.at[dst_r, dst_c]),
-                    (nw.at[src_r, src_c], wgt.at[dst_r, dst_c]),
-                )
-            ):
-                copy = pltpu.make_async_remote_copy(
-                    src_ref=src,
-                    dst_ref=dst,
-                    send_sem=halo_send.at[index * 3 + j],
-                    recv_sem=halo_recv.at[index * 3 + j],
-                    device_id=at(dr, dc),
-                    device_id_type=MESH,
-                )
-                trio.append(copy)
-            halo[dr, dc] = trio
-    for key in ((0, 1), (0, -1), (1, 1), (1, -1), (-1, 1), (-1, -1), (1, 0), (-1, 0)):
-        for copy in halo[key]:
-            copy.start()
-    for copy in local:
+    for n, side in enumerate(("up", "down")):
+
+        @pl.when(jnp.logical_not(has[side]))
+        def _(n=n):
+            band_in[n] = jnp.zeros(band_in.shape[1:], bf16)
+            corner_in[2 * n] = jnp.zeros(corner_in.shape[1:], bf16)
+            corner_in[2 * n + 1] = jnp.zeros(corner_in.shape[1:], bf16)
+
+    for n, side in enumerate(("left", "right")):
+
+        @pl.when(jnp.logical_not(has[side]))
+        def _(n=n):
+            strip_in[n] = jnp.zeros(strip_in.shape[1:], bf16)
+
+    for copy in local[:3]:
         copy.wait()
-    for key in halo:
-        for copy in halo[key]:
-            copy.wait()
-
-    for block, first, last, base in ((0, rows - HALO, rows, 0), (1, 0, rows, HALO), (2, 0, HALO, HALO + rows)):
-        def turned(slot):
-            flat = jnp.where(nbx[slot] >= 0, 1.0, 0.0).astype(jnp.float32).reshape(slots * rows, cols)
-            return jnp.transpose(flat)
-
-        whole = jnp.concatenate(
-            [turned(3 * block)[cols - SIDE :], turned(3 * block + 1), turned(3 * block + 2)[:SIDE]], axis=0
+    flat = jnp.where(own_nb[...] >= 0, 1.0, 0.0).astype(f32).reshape(slots * rows, cols)
+    flat = jnp.concatenate([flat, jnp.zeros((128 - slots * rows, cols), f32)], axis=0)
+    turned = jnp.transpose(flat)
+    listed = jnp.concatenate([turned, jnp.zeros((cols, pix - 128), f32)], axis=1)
+    half = rows // 2 - 1
+    unit, small = 2 * cols, 2 * SIDE
+
+    def spot(row, size, middle):
+        return row * size + (middle if row >= half else 0)
+
+    band_out[pl.ds(half * unit, cols), :] = listed.astype(bf16)
+    for n, c0 in ((0, 0), (1, cols - SIDE)):
+        strip_out[n, pl.ds(half * small, small), :] = jnp.concatenate(
+            [listed[c0 : c0 + SIDE], jnp.zeros((SIDE, pix), f32)], axis=0
+        ).astype(bf16)
+    for row in range(rows):
+        r = res[HALO + row, pl.ds(SIDE, cols), :]
+        w = wgt[HALO + row, pl.ds(SIDE, cols), :] - MIDDLE
+        band_out[pl.ds(spot(row, unit, cols), unit), :] = jnp.concatenate([r, w], axis=0).astype(bf16)
+        for n, c0 in ((0, 0), (1, cols - SIDE)):
+            strip_out[n, pl.ds(spot(row, small, small), small), :] = jnp.concatenate(
+                [r[c0 : c0 + SIDE], w[c0 : c0 + SIDE]], axis=0
+            ).astype(bf16)
+
+    band_size = HALO * unit + cols
+    corner_size = HALO * small + small
+
+    def remote(src, dst, index, peer):
+        return pltpu.make_async_remote_copy(
+            src_ref=src, dst_ref=dst, send_sem=h_send.at[index], recv_sem=h_recv.at[index],
+            device_id=peer, device_id_type=MESH,
         )
+
+    far_band, far_strip = pl.ds((rows - HALO) * unit, band_size), pl.ds((rows - HALO) * small, corner_size)
+    near_band, near_strip = pl.ds(0, band_size), pl.ds(0, corner_size)
+    strips = [
+        ("right", "left", lambda: remote(strip_out.at[1], strip_in.at[0], 0, beside["right"])),
+        ("left", "right", lambda: remote(strip_out.at[0], strip_in.at[1], 1, beside["left"])),
+    ]
+    bands = [
+        ("down", "up", lambda: remote(band_out.at[far_band], band_in.at[0], 2, beside["down"])),
+        ("up", "down", lambda: remote(band_out.at[near_band], band_in.at[1], 3, beside["up"])),
+    ]
+    corners = [
+        [
+            ("down", "up", lambda n=n: remote(strip_in.at[n, far_strip], corner_in.at[n], 4 + n, beside["down"])),
+            ("up", "down", lambda n=n: remote(strip_in.at[n, near_strip], corner_in.at[2 + n], 6 + n, beside["up"])),
+        ]
+        for n in range(2)
+    ]
+
+    def each(copies, act, by):
+        for entry in copies:
+
+            @pl.when(has[entry[by]])
+            def _(entry=entry):
+                getattr(entry[2](), act)()
+
+    amount = 7
+    for side in sides:
+        amount = amount + jnp.where(has[side], 1, 0)
+    pl.semaphore_wait(barrier, amount)
+    each(strips, "start", 0)
+    each(bands, "start", 0)
+    for n in range(2):
+        each(strips[n : n + 1], "wait_recv", 1)
+        each(corners[n], "start", 0)
+    each(bands, "wait_recv", 1)
+    for n in range(2):
+        each(corners[n], "wait_recv", 1)
+
+    for n, base in ((0, 0), (1, HALO + rows)):
+        skip = (rows - HALO) if n == 0 else 0
+        for i in range(HALO):
+            row = i + skip
+            o = spot(row, unit, cols) - skip * unit
+            part = band_in[n, pl.ds(o, unit), :].astype(f32)
+            res[base + i, pl.ds(SIDE, cols), :] = part[:cols]
+            wgt[base + i, pl.ds(SIDE, cols), :] = part[cols:] + MIDDLE
+            o = spot(row, small, small) - skip * small
+            for m, c0 in ((0, 0), (1, SIDE + cols)):
+                part = corner_in[2 * n + m, pl.ds(o, small), :].astype(f32)
+                res[base + i, pl.ds(c0, SIDE), :] = part[:SIDE]
+                wgt[base + i, pl.ds(c0, SIDE), :] = part[SIDE:] + MIDDLE
+    for m, c0 in ((0, 0), (1, SIDE + cols)):
+        for row in range(rows):
+            part = strip_in[m, pl.ds(spot(row, small, small), small), :].astype(f32)
+            res[HALO + row, pl.ds(c0, SIDE), :] = part[:SIDE]
+            wgt[HALO + row, pl.ds(c0, SIDE), :] = part[SIDE:] + MIDDLE
+
+    above, below = (half - rows + HALO), half
+    for first, last, base, left, mid, right in (
+        (
+            rows - HALO, rows, 0,
+            corner_in[0, pl.ds(above * small, small), :], band_in[0, pl.ds(above * unit, cols), :],
+            corner_in[1, pl.ds(above * small, small), :],
+        ),
+        (
+            0, rows, HALO,
+            strip_in[0, pl.ds(half * small, small), :], None, strip_in[1, pl.ds(half * small, small), :],
+        ),
+        (
+            0, HALO, HALO + rows,
+            corner_in[2, pl.ds(below * small, small), :], band_in[1, pl.ds(below * unit, cols), :],
+            corner_in[3, pl.ds(below * small, small), :],
+        ),
+    ):
+        middle = turned if mid is None else mid.astype(f32)[:, :128]
+        whole = jnp.concatenate([left.astype(f32)[:SIDE, :128], middle, right.astype(f32)[:SIDE, :128]], axis=0)
         for k in range(slots):
             for row in range(first, last):
                 m = k * rows + row
-                wide = jnp.broadcast_to(whole[:, m : m + 1], (ext_cols, 128)).astype(jnp.bfloat16)
+                wide = jnp.broadcast_to(whole[:, m : m + 1], (ext_cols, 128)).astype(bf16)
                 msk[k, pl.ds((base + row - first) * ext_cols, ext_cols), :] = wide
+    local[3].wait()
 
     center, steps = coefficients()
 
@@ -193,42 +283,69 @@
         low_part, fold, preferred_element_type=jnp.float32
     )
     quarter = (rows // 2) * (cols // 2)
-    y = [summed[q * quarter : (q + 1) * quarter] for q in range(4)]
+    quads = [summed[q * quarter : (q + 1) * quarter] for q in range(4)]
     left = lax.broadcasted_iota(jnp.int32, (quarter, 128), 1) < 64
-    coarse = jnp.concatenate([jnp.where(left, y[0], y[1]), jnp.where(left, y[2], y[3])], axis=1).astype(jnp.bfloat16)
-    mine = pl.ds(pl.multiple_of(fcol * (cols // 2), cols // 2), cols // 2)
-    out_ref[:, mine, :] = coarse.reshape(rows // 2, cols // 2, pix)
-
-    def given(i):
+    coarse = jnp.concatenate([jnp.where(left, quads[0], quads[1]), jnp.where(left, quads[2], quads[3])], axis=1).astype(jnp.bfloat16)
+    quarter_cols = cols // 2
+    group = rows // 4
+
+    def block(j, half=None):
+        span = pl.ds(pl.multiple_of(j * quarter_cols, quarter_cols), quarter_cols)
+        if half is None:
+            return out_ref.at[:, span, :]
+        return out_ref.at[pl.ds(half * group, group), span, :]
+
+    out_ref[:, pl.ds(pl.multiple_of(fcol * quarter_cols, quarter_cols), quarter_cols), :] = coarse.reshape(
+        rows // 2, quarter_cols, pix
+    )
+
+    def move(ref, index, peer):
         return pltpu.make_async_remote_copy(
-            src_ref=out_ref.at[:, mine, :],
-            dst_ref=out_ref.at[:, mine, :],
-            send_sem=g_send.at[i],
-            recv_sem=g_recv.at[i],
-            device_id=(frow, lax.rem(fcol + i, n_col)),
-            device_id_type=MESH,
+            src_ref=ref, dst_ref=ref, send_sem=g_send.at[index], recv_sem=g_recv.at[index],
+            device_id=(frow, peer), device_id_type=MESH,
         )
 
-    def start(i, c):
-        given(i).start()
-        return c
-
-    def finish(i, c):
-        other = lax.rem(fcol - i + n_col, n_col)
-        theirs = pl.ds(pl.multiple_of(other * (cols // 2), cols // 2), cols // 2)
-        pltpu.make_async_remote_copy(
-            src_ref=out_ref.at[:, theirs, :],
-            dst_ref=out_ref.at[:, theirs, :],
-            send_sem=g_send.at[i],
-            recv_sem=g_recv.at[i],
-            device_id=(frow, lax.rem(fcol + i, n_col)),
-            device_id_type=MESH,
-        ).wait_recv()
-        given(i).wait_send()
-        return c
-
-    lax.fori_loop(1, n_col, start, 0)
-    lax.fori_loop(1, n_col, finish, 0)
+    routes = ((along_x, along_y), (along_y, along_x))
+
+    def source(way, d, which):
+        return way((4 - d) % 4) + which * (4 - 8 * zh)
+
+    def index_of(which, half, d1, d2):
+        return 1 + ((which * 2 + half) * 4 + d1) * 4 + d2
+
+    sent = [move(block(fcol), 0, partner)]
+    sent[0].start()
+    near = (1, 3, 2)
+    for which in range(2):
+        base = fcol + which * (4 - 8 * zh)
+        if which == 1:
+            move(block(base), 0, partner).wait_recv()
+        for stage in range(2):
+            for half in range(2):
+                for d in near:
+                    key = index_of(which, half, d, 0) if stage == 0 else index_of(which, half, 0, d)
+                    copy = move(block(base, half), key, routes[half][stage](d))
+                    copy.start()
+                    sent.append(copy)
+        for d1 in near:
+            for half in range(2):
+                ref = block(source(routes[half][0], d1, which), half)
+                move(ref, index_of(which, half, d1, 0), fcol).wait_recv()
+                for d2 in near:
+                    copy = move(ref, index_of(which, half, d1, d2), routes[half][1](d2))
+                    copy.start()
+                    sent.append(copy)
+    for which in range(2):
+        for half in range(2):
+            for d1 in (0,) + near:
+                for d2 in near:
+                    move(block(fcol, half), index_of(which, half, d1, d2), fcol).wait_recv()
+    for copy in sent:
+        copy.wait_send()
+    each(strips, "wait_send", 0)
+    each(bands, "wait_send", 0)
+    for n in range(2):
+        each(corners[n], "wait_send", 0)
 
 
 CHUNK = (9, 8, 7, 6, 5, 8)
@@ -257,19 +374,24 @@
                 pltpu.VMEM((tiles, pix), jnp.float32),
                 pltpu.VMEM((2, 3, tiles, pix), jnp.bfloat16),
                 pltpu.VMEM((slots, tiles, 128), jnp.bfloat16),
-                pltpu.VMEM((9, slots, rows, cols), jnp.int32),
+                pltpu.VMEM((pix // 128, rows * ext[1], 128), jnp.float32),
+                pltpu.VMEM((slots, rows, cols), jnp.int32),
                 pltpu.VMEM((slots, pix, pix), jnp.bfloat16),
-                pltpu.VMEM((pix // 128, rows * ext[1], 128), jnp.float32),
-                pltpu.SemaphoreType.DMA((24,)),
-                pltpu.SemaphoreType.DMA((24,)),
+                pltpu.VMEM((2 * rows * cols + cols, pix), jnp.bfloat16),
+                pltpu.VMEM((2, 2 * HALO * cols + cols, pix), jnp.bfloat16),
+                pltpu.VMEM((2, 2 * rows * SIDE + 2 * SIDE, pix), jnp.bfloat16),
+                pltpu.VMEM((2, 2 * rows * SIDE + 2 * SIDE, pix), jnp.bfloat16),
+                pltpu.VMEM((4, 2 * HALO * SIDE + 2 * SIDE, pix), jnp.bfloat16),
                 pltpu.SemaphoreType.DMA((4,)),
-                pltpu.SemaphoreType.DMA((n_col,)),
-                pltpu.SemaphoreType.DMA((n_col,)),
+                pltpu.SemaphoreType.DMA((8,)),
+                pltpu.SemaphoreType.DMA((8,)),
+                pltpu.SemaphoreType.DMA((65,)),
+                pltpu.SemaphoreType.DMA((65,)),
             ],
             compiler_params=pltpu.CompilerParams(
                 collective_id=0, has_side_effects=True, vmem_limit_bytes=48 << 20
             ),
-        )(right_side, noise_weight, stencils, listed)
+        )(*[pltpu.with_memory_space_constraint(v, pltpu.HBM) for v in (right_side, noise_weight, stencils, listed)])
         return smooth, coarse.astype(jnp.float32)
 
     placed = (P("frow", "fcol", None), P("frow", "fcol", None), P(), P("frow", "fcol", None))

time: 82.6 us -> 48.2 us (0.58)
  the two profiles are of different devices: /device:TPU:121 before, /device:TPU:1 now
where the time goes in v2:
time: 48.2 us; the launch traced here: 48.1 us
  Pallas kernels  45.3 us (94%)
  other arithmetic  1.5 us (3%)
  local copies, waits for them, and re-layouts  0.7 us (1%)
  between operations  0.64 us (1%)
    pallas_call x1, Pallas kernels, body(): pl.pallas_call(functools.partial(kernel, (n_row, n_col, rows, cols, pix,...  45.3 us
    convert_element_type x1, other arithmetic, body(): return (smooth, coarse.astype(jnp.float32))  1.5 us

profile of v2, /device:TPU:1, one launch (start us, length us, event | category | flops | bytes accessed | tf_op | source)
XLA Modules:
  0.0 48.1 jit_solution(1012536766536226693)
XLA Ops:
  0.6 45.3 %shard_map.59 = (f32[8,32,256]{2,1,0:T(8,128)S(1)}, bf16[4,512,256]{2,1,0:T(8,128)(2,1)S(1)}) custom-call(f32[8,32,256]{2,1,0:T(8,128)} %rs.1, f32[8,32,256]{2,1,0:T(8,128)} %nw.1, bf16[9,256,256]{2,1,0:T(8,128)(2,1)} %st.1, s32[9,8,32]{2,1,0:T(8,128)} %bitcast.1), custom_call_target="tpu_custom_call" | custom-call | tf_op jit(solution)/shard_map/pallas_call | solution.py:363
  45.9 1.5 %convert_element_type.3 = f32[4,512,256]{2,1,0:T(8,128)} convert(bf16[4,512,256]{2,1,0:T(8,128)(2,1)S(1)} %get-tuple-element.5) | non-fusion elementwise | flops 524288 | bytes 3145728 | tf_op jit(solution)/shard_map/convert_element_type | solution.py:395
  47.4 0.7 %copy.7 = f32[8,32,256]{2,1,0:T(8,128)} copy(f32[8,32,256]{2,1,0:T(8,128)S(1)} %get-tuple-element.8) | data formatting | bytes 524288
